TPU v7x, 32 devices: a whole 2x2x4 slice. The times are simulated.
32 devices in a mesh: grp: 4 (over z), ch: 8 (over y, x, core).
Axes of the slice: x: 2, y: 2, z: 4, core: 2. Of those that a mesh axis runs over, the one named last changes fastest.
Arguments:
- features: bfloat16 [64, 64, 512], P(('grp', 'ch')), may hold values from -6 to 6
- live_counts: int32 [32], P(('grp', 'ch')), may hold values from 1 to 2, as said below
- neighbours: int32 [64, 27], P(('grp', 'ch')), may hold values from -1 to 63, as said below
- w_first: bfloat16 [27, 64, 64], replicated, may hold values from -0.21875 to 0.21875
- w_second: bfloat16 [27, 64, 64], replicated, may hold values from -0.21875 to 0.21875
- w_middle: bfloat16 [27, 128, 64], replicated, may hold values from -0.3125 to 0.3125
- w_coarse: bfloat16 [27, 256, 128], P(None, 'ch'), may hold values from -0.21875 to 0.21875
- w_project: bfloat16 [256, 64], P('ch'), may hold values from -0.75 to 0.75
- w_output: bfloat16 [64, 128], replicated, may hold values from -0.5 to 0.5
Outputs:
- mixed_out: bfloat16 [64, 64, 512], P(('grp', 'ch'))
Inputs may be any that keep to these rules, and one draw needn't show every extreme that they name: Device d holds its live blocks in slots d * 2 to d * 2 + live_counts[d] - 1; the rest are padding. In every group of devices along ch one device holds exactly 2. `neighbours`: the live blocks occupy distinct positions of a lattice of 16 x 16 x (2 times the size of grp) positions; the devices with grp index g hold exactly the blocks of layers g * 2 to (g + 1) * 2 - 1 along z. Within a group, the device with ch index m (of n) holds blocks only in the tile of x from floor(2 m / n) * 8 to that plus 16 / 2 - 1 and y from (m mod (n / 2)) * 2 * 16 / n to that plus 2 * 16 / n - 1. For a live block b, entry 9 (dx + 1) + 3 (dy + 1) + dz + 1 is the block at b's position plus (dx, dy, dz), or -1 where that position is empty or off the lattice; entry 13 is b itself. Rows of padding slots are all -1, and no entry names a padding slot.
All inputs are finite; a program needn't handle non-finite values.
Results may differ from a plain program's by a relative error of at most 0.013.
Values may be sent and summed in bfloat16 or wider, within the bound.
A program may use at most 128 MiB of HBM per device.

v0:
```python
import functools

import jax
import jax.numpy as jnp
from jax import lax
from jax.experimental import pallas as pl
from jax.experimental.pallas import tpu as pltpu
from jax.sharding import PartitionSpec as P

MESH = pl.DeviceIdType.MESH
F32, BF16 = jnp.float32, jnp.bfloat16
STEPS = (-1, 0, 1)
OFFSETS = [(x, y, z) for x in STEPS for y in STEPS for z in STEPS]
PARTNERS = [(h, y, z) for h in (0, 1) for y in STEPS for z in STEPS if (h, y, z) != (0, 0, 0)]
PIECES = 3


def matmul_nt(left, right):
    return lax.dot_general(left, right, (((1,), (1,)), ((), ())), preferred_element_type=F32)


def rounded_gelu(value):
    return jax.nn.gelu(value).astype(BF16)


def kernel(grps, n, feat_any, live, neigh, w1_any, w2_any, wm_any, wc_any, wp_any, wo_any, out, levels, mats, sems):
    g, m = lax.axis_index("grp"), lax.axis_index("ch")
    q = n // 2
    half, tile = m // q, m % q
    slots, c0, voxels = feat_any.shape
    edge = round(voxels ** (1 / 3))
    c1 = wm_any.shape[2]

    def has(partner):
        _, y, z = partner
        return (tile + y >= 0) & (tile + y < q) & (g + z >= 0) & (g + z < grps)

    def coords(partner):
        h, y, z = partner
        return g + z, ((1 - half) if h else half) * q + tile + y

    barrier = pltpu.get_barrier_semaphore()
    for r in range(1, n):
        pl.semaphore_signal(barrier, inc=1, device_id=(g, (m + r) % n), device_id_type=MESH)
    far = [p for p in PARTNERS if p[2] != 0]
    for p in far:

        @pl.when(has(p))
        def _():
            pl.semaphore_signal(barrier, inc=1, device_id=coords(p), device_id_type=MESH)

    (feat, w1, w2, wm, wo, wc, wp, b1, b2, bm, im_leaf, im_mid, im_coarse) = mats
    (local_sem, wsend, wrecv, psend, precv) = sems
    loads = [
        pltpu.make_async_copy(source, target, local_sem.at[i])
        for i, (source, target) in enumerate(
            [(w1_any, w1), (w2_any, w2), (wm_any, wm), (wo_any, wo), (wc_any, wc.at[m]), (wp_any, wp.at[m]), (feat_any, feat)]
        )
    ]
    for load in loads[-1:] + loads[:-1]:
        load.start()

    def piece_of(level, partner):
        h, y, z = partner
        volume, caps = level["v"], level["caps"]
        length = volume.shape[0]
        pick_x = pl.ds((1 - half) * (length - 1), 1) if h else slice(None)
        pick_y = slice(None) if y == 0 else (pl.ds(length - 1, 1) if y > 0 else pl.ds(0, 1))
        if z == 0:
            return volume.at[pick_x, pick_y]
        return caps.at[1 if z > 0 else 0, pick_x, pick_y]

    def copy_to(level, index):
        h, y, z = PARTNERS[index]
        back = PARTNERS.index((h, -y, -z))
        return pltpu.make_async_remote_copy(
            src_ref=piece_of(level, PARTNERS[index]),
            dst_ref=level["got"][back],
            send_sem=level["send"].at[index],
            recv_sem=level["recv"].at[back],
            device_id=coords(PARTNERS[index]),
            device_id_type=MESH,
        )

    order = sorted(range(len(PARTNERS)), key=lambda i: -sum(abs(s) for s in PARTNERS[i]))

    def caps_of(level):
        volume, caps = level["v"], level["caps"]
        length = volume.shape[0]
        caps[0] = volume[:, :, 0:1, :]
        caps[1] = volume[:, :, length - 1 : length, :]

    def send(level):
        for i in order:

            @pl.when(has(PARTNERS[i]))
            def _():
                copy_to(level, i).start()

    def receive(level):
        for i in order:
            h, y, z = PARTNERS[i]

            @pl.when(has((h, -y, -z)))
            def _():
                copy_to(level, i).wait_recv()

    def extend(level):
        volume, ext, caps = level["v"], level["ext"], level["caps"]
        length, lanes = volume.shape[0], volume.shape[3]
        middle = lanes // 2
        lane = lax.broadcasted_iota(jnp.int32, (1, 1, 1, lanes), 3)
        upper = (lane >= middle).astype(jnp.int32)
        ext[1 : length + 1, 1 : length + 1, 1 : length + 1, :] = volume[...]
        firsts = {}
        for p in [(0, 0, 0)] + PARTNERS:
            a, b = coords(p)
            firsts[p] = jnp.where(has(p), (a * n + b) * 2, -8)

        def source_at(step):
            return slice(0, length) if step == 0 else (slice(0, 1) if step > 0 else slice(length - 1, length))

        def target_at(step):
            return slice(1, length + 1) if step == 0 else (slice(0, 1) if step < 0 else slice(length + 1, length + 2))

        for column, (x, y, z) in enumerate(OFFSETS):
            if (x, y, z) == (0, 0, 0):
                continue
            wanted = jnp.where(upper == 1, neigh[1, column], neigh[0, column])
            shape = tuple(length if s == 0 else 1 for s in (x, y, z)) + (lanes,)
            wanted = jnp.broadcast_to(wanted, shape)
            upper_full = jnp.broadcast_to(upper, shape)
            value = jnp.zeros(shape, F32)
            for h in (0, 1) if x else (0,):
                for cy in (0, y) if y else (0,):
                    for cz in (0, z) if z else (0,):
                        p = (h, cy, cz)
                        at_x = slice(0, 1) if h else source_at(x)
                        at_y = slice(0, 1) if cy else source_at(y)
                        at_z = slice(0, 1) if cz else source_at(z)
                        if p == (0, 0, 0):
                            if z:
                                found = caps[0 if z > 0 else 1, at_x, at_y, :, :]
                            else:
                                found = volume[at_x, at_y, at_z, :]
                        else:
                            found = level["got"][PARTNERS.index(p)][at_x, at_y, at_z, :]
                        swapped = jnp.concatenate([found[..., middle:], found[..., :middle]], axis=3)
                        value = jnp.where(
                            wanted == firsts[p] + upper_full,
                            found,
                            jnp.where(wanted == firsts[p] + 1 - upper_full, swapped, value),
                        )
            ext[target_at(x), target_at(y), target_at(z), :] = value

    taps = wc.shape[1]

    pairs = n // 2
    pair, core = m // 2, m % 2
    partner = pair * 2 + 1 - core

    def weight_copies(part, role, r):
        first, last = taps * part // PIECES, taps * (part + 1) // PIECES
        other = (pair + pairs - r) % pairs * 2
        owner, came = [(m, partner), (m, other + core), (other + core, other + 1 - core)][role]
        target = (pair + r) % pairs * 2 + core if role == 1 else partner
        lane = (0, r, pairs - 1 + r)[role]

        def copy(who):
            spot = wc.at[who, pl.ds(first, last - first)]
            return pltpu.make_async_remote_copy(
                src_ref=spot,
                dst_ref=spot,
                send_sem=wsend.at[part, lane],
                recv_sem=wrecv.at[part, lane],
                device_id=(g, target),
                device_id_type=MESH,
            )

        return functools.partial(copy, owner), functools.partial(copy, came)

    def project_copy(r, other):
        return pltpu.make_async_remote_copy(
            src_ref=wp.at[other],
            dst_ref=wp.at[other],
            send_sem=psend.at[r - 1],
            recv_sem=precv.at[r - 1],
            device_id=(g, (m + r) % n),
            device_id_type=MESH,
        )

    def send_weights(part):
        for r in range(1, pairs):
            weight_copies(part, 1, r)[0]().start()
        weight_copies(part, 0, 0)[0]().start()

    def hand_on(part):
        for r in range(1, pairs):
            weight_copies(part, 1, r)[1]().wait_recv()
            weight_copies(part, 2, r)[0]().start()

    def diagonal(matrix):
        empty = jnp.zeros_like(matrix)
        return jnp.concatenate([matrix, empty], axis=1), jnp.concatenate([empty, matrix], axis=1)

    def fill_diagonal(weights, target):
        rows, width = weights.shape[1], 2 * weights.shape[2]
        for t in range(weights.shape[0]):
            top, bottom = diagonal(weights[t])
            at = (t % 9) * width
            target[t // 9, 0:rows, at : at + width] = top
            target[t // 9, rows : 2 * rows, at : at + width] = bottom

    def fill_upright(weights, target):
        rows, width = weights.shape[1:]
        for t in range(weights.shape[0]):
            empty = jnp.zeros((rows, width), BF16)
            for b in range(slots):
                at = (t % 9 * slots + b) * rows
                for other in range(slots):
                    there = weights[t] if other == b else empty
                    target[t // 9, at : at + rows, other * width : (other + 1) * width] = there

    def convolve_leaf(level, weights):
        ext, length, lanes = level["ext"], edge, level["v"].shape[3]
        for k in range(9):
            y, z = k // 3, k % 3
            rows = ext[:, y : y + length, z : z + length, :].reshape(length + 2, length * length, lanes)
            im_leaf[:, :, k * lanes : (k + 1) * lanes] = rows.astype(BF16)
        total = None
        for x in range(3):
            window = im_leaf[x : x + length].reshape(length**3, 9 * lanes)
            term = matmul_nt(window, weights[x])
            total = term if total is None else total + term
        return rounded_gelu(total)

    leaf_a, leaf_b, mid, low = levels
    loads[-1].wait()
    packed = feat[...].reshape(slots * c0, voxels).astype(F32)
    leaf_a["v"][...] = packed.T.reshape(edge, edge, edge, slots * c0)
    caps_of(leaf_a)
    peers = n - 1
    for p in far:
        peers = peers + has(p).astype(jnp.int32)
    pl.semaphore_wait(barrier, peers)

    send(leaf_a)
    loads[0].wait()
    fill_diagonal(w1, b1)
    loads[4].wait()
    loads[5].wait()
    send_weights(0)
    for r in range(1, n):
        project_copy(r, m).start()
    receive(leaf_a)
    send_weights(1)
    extend(leaf_a)
    first = convolve_leaf(leaf_a, b1)

    leaf_b["v"][...] = first.astype(F32).reshape(edge, edge, edge, slots * c0)
    caps_of(leaf_b)
    send(leaf_b)
    loads[1].wait()
    fill_diagonal(w2, b2)
    hand_on(0)
    receive(leaf_b)
    send_weights(2)
    extend(leaf_b)
    second = convolve_leaf(leaf_b, b2)

    def halving(length):
        small = length // 2
        row = lax.broadcasted_iota(jnp.int32, (small**3, length**3), 0)
        column = lax.broadcasted_iota(jnp.int32, (small**3, length**3), 1)
        x, y, z = column // (length * length), column // length % length, column % length
        hit = row == (x // 2) * small * small + (y // 2) * small + z // 2
        return jnp.where(hit, 0.125, 0.0).astype(BF16)

    side = edge // 2
    pooled = jnp.dot(halving(edge), second, preferred_element_type=F32).astype(BF16).astype(F32)
    for x in range(side):
        for y in range(side):
            at = (x * side + y) * side
            mid["v"][x, y] = pooled[at : at + side]
    caps_of(mid)
    send(mid)
    loads[2].wait()
    fill_upright(wm, bm)
    hand_on(1)
    receive(mid)
    extend(mid)
    lanes = slots * c0
    for k in range(9):
        ty, tz = k // 3, k % 3
        for y in range(side):
            im_mid[:, y * side : (y + 1) * side, k * lanes : (k + 1) * lanes] = mid["ext"][:, y + ty, tz : tz + side, :]
    total = None
    for x in range(3):
        window = im_mid[x : x + side].astype(BF16).reshape(side**3, 9 * lanes)
        term = jnp.dot(window, bm[x], preferred_element_type=F32)
        total = term if total is None else total + term
    middle = rounded_gelu(total)

    small = side // 2
    pooled = jnp.dot(halving(side), middle, preferred_element_type=F32).astype(BF16).astype(F32)
    for x in range(small):
        for y in range(small):
            at = (x * small + y) * small
            low["v"][x, y] = pooled[at : at + small]
    caps_of(low)
    send(low)
    loads[3].wait()
    skip_top, skip_bottom = diagonal(wo[:, :c0])
    lift_top, lift_bottom = diagonal(wo[:, c0:])
    skip_weights = jnp.concatenate([skip_top, skip_bottom], axis=0)
    lift_weights = jnp.concatenate([lift_top, lift_bottom], axis=0)
    mixed = matmul_nt(skip_weights, second)
    hand_on(2)
    for part in range(PIECES):
        weight_copies(part, 0, 0)[1]().wait_recv()
        for r in range(1, pairs):
            weight_copies(part, 2, r)[1]().wait_recv()
    for r in range(1, n):
        project_copy(r, (m + n - r) % n).wait_recv()
    receive(low)
    extend(low)
    cells = small**3
    for t in range(taps):
        tx, ty, tz = t // 9, t // 3 % 3, t % 3
        for b in range(slots):
            for x in range(small):
                for y in range(small):
                    at = b * cells + (x * small + y) * small
                    im_coarse[at : at + small, t * c1 : (t + 1) * c1] = low["ext"][
                        x + tx, y + ty, tz : tz + small, b * c1 : (b + 1) * c1
                    ]
    total = None
    c2 = n * wc.shape[2]
    for t in range(taps):
        term = matmul_nt(im_coarse[:, t * c1 : (t + 1) * c1].astype(BF16), wc[:, t].reshape(c2, c1))
        total = term if total is None else total + term
    hidden = rounded_gelu(total)
    coarse = jnp.dot(hidden, wp[...].reshape(c2, c0), preferred_element_type=F32)
    coarse = jnp.concatenate([coarse[b * cells : (b + 1) * cells] for b in range(slots)], axis=1).astype(BF16)
    row = lax.broadcasted_iota(jnp.int32, (voxels, cells), 0)
    column = lax.broadcasted_iota(jnp.int32, (voxels, cells), 1)
    factor = edge // small
    x, y, z = row // (edge * edge), row // edge % edge, row % edge
    spread = column == (x // factor) * small * small + (y // factor) * small + z // factor
    spread = jnp.where(spread, 1.0, 0.0).astype(BF16)
    widened = jnp.dot(spread, coarse, preferred_element_type=F32).astype(BF16)
    mixed = mixed + matmul_nt(lift_weights, widened)
    owner = lax.broadcasted_iota(jnp.int32, mixed.shape, 0) // c0
    mixed = jnp.where(owner < live[0], mixed, 0.0).astype(BF16)
    for b in range(slots):
        out[b] = mixed[b * c0 : (b + 1) * c0]

    for level in levels:
        for i in order:

            @pl.when(has(PARTNERS[i]))
            def _():
                copy_to(level, i).wait_send()

    for r in range(1, n):
        project_copy(r, m).wait_send()
    for part in range(PIECES):
        weight_copies(part, 0, 0)[0]().wait_send()
        for r in range(1, pairs):
            weight_copies(part, 1, r)[0]().wait_send()
            weight_copies(part, 2, r)[0]().wait_send()


def level_scratch(length, lanes):
    def got(partner):
        h, y, z = partner
        return pltpu.VMEM((1 if h else length, 1 if y else length, 1 if z else length, lanes), F32)

    return dict(
        v=pltpu.VMEM((length, length, length, lanes), F32),
        caps=pltpu.VMEM((2, length, length, 1, lanes), F32),
        ext=pltpu.VMEM((length + 2,) * 3 + (lanes,), F32),
        got=[got(p) for p in PARTNERS],
        send=pltpu.SemaphoreType.DMA((len(PARTNERS),)),
        recv=pltpu.SemaphoreType.DMA((len(PARTNERS),)),
    )


def shards(grps, n, features, live_counts, neighbours, w_first, w_second, w_middle, w_coarse, w_project, w_output):
    slots, c0, voxels = features.shape
    edge = round(voxels ** (1 / 3))
    w_middle = jnp.swapaxes(w_middle, 1, 2)
    taps, _, c1 = w_middle.shape
    lanes = slots * c0
    side, small = edge // 2, edge // 4
    levels = [
        level_scratch(edge, lanes),
        level_scratch(edge, lanes),
        level_scratch(side, lanes),
        level_scratch(small, slots * c1),
    ]
    mats = [
        pltpu.VMEM(features.shape, BF16),
        pltpu.VMEM(w_first.shape, BF16),
        pltpu.VMEM(w_second.shape, BF16),
        pltpu.VMEM(w_middle.shape, BF16),
        pltpu.VMEM(w_output.shape, BF16),
        pltpu.VMEM((n,) + w_coarse.shape, BF16),
        pltpu.VMEM((n,) + w_project.shape, BF16),
        pltpu.VMEM((3, lanes, 9 * lanes), BF16),
        pltpu.VMEM((3, lanes, 9 * lanes), BF16),
        pltpu.VMEM((3, 9 * lanes, slots * c1), BF16),
        pltpu.VMEM((edge + 2, edge * edge, 9 * lanes), BF16),
        pltpu.VMEM((side + 2, side * side, 9 * lanes), F32),
        pltpu.VMEM((slots * small**3, taps * c1), F32),
    ]
    sems = [
        pltpu.SemaphoreType.DMA((7,)),
        pltpu.SemaphoreType.DMA((PIECES, n - 1)),
        pltpu.SemaphoreType.DMA((PIECES, n - 1)),
        pltpu.SemaphoreType.DMA((n - 1,)),
        pltpu.SemaphoreType.DMA((n - 1,)),
    ]
    smem = pl.BlockSpec(memory_space=pltpu.SMEM)
    vmem = pl.BlockSpec(memory_space=pltpu.VMEM)
    stay = pl.BlockSpec(memory_space=pl.ANY)
    return pl.pallas_call(
        functools.partial(kernel, grps, n),
        out_shape=jax.ShapeDtypeStruct(features.shape, BF16),
        in_specs=[stay, smem, smem] + [stay] * 6,
        out_specs=vmem,
        scratch_shapes=[levels, mats, sems],
        compiler_params=pltpu.CompilerParams(collective_id=0, has_side_effects=True),
    )(features, live_counts, neighbours, w_first, w_second, w_middle, w_coarse, w_project, w_output)


def solution(mesh):
    in_specs = (
        P(("grp", "ch"), None, None),
        P(("grp", "ch")),
        P(("grp", "ch"), None),
        P(),
        P(),
        P(),
        P(None, "ch", None),
        P("ch", None),
        P(),
    )
    return jax.shard_map(
        functools.partial(shards, mesh.shape["grp"], mesh.shape["ch"]),
        mesh=mesh,
        in_specs=in_specs,
        out_specs=P(("grp", "ch"), None, None),
        check_vma=False,
    )
```

profile of v0, /device:TPU:0, one launch (start us, length us, event | category | flops | bytes accessed | tf_op | source)
XLA Modules:
  0.0 32.3 jit_solution(2621496032095873106)
XLA Ops:
  0.7 30.0 %shard_map.91 = bf16[2,64,512]{2,1,0:T(8,128)(2,1)} custom-call(bf16[2,64,512]{2,1,0:T(8,128)(2,1)} %feat_any.1, s32[1]{0:T(128)S(6)} %copy.11.live, s32[2,27]{1,0:T(2,128)} %neigh.1, bf16[27,64,64]{2,1,0:T(8,128)(2,1)} %w1_any.1, bf16[27,64,64]{2,1,0:T(8,128)(2,1)} %w2_any.1, bf16[27,64,128]{2,1,0:T(8,128)(2,1)} %bitcast.1, bf16[27,32,128]{2,1,0:T(8,128)(2,1)} %wc_any.1, ...), custom_call_target="tpu_custom_call" | custom-call | tf_op jit(solution)/shard_map/pallas_call | solution.py:427
  30.7 1.6 %copy.12 = bf16[2,64,512]{2,1,0:T(8,128)(2,1)} copy(bf16[2,64,512]{2,1,0:T(8,128)(2,1)} %shard_map.91) | data formatting | bytes 262144
where the time goes:
time: 32.5 us; the launch traced here: 32.3 us
  Pallas kernels  30 us (92%)
  local copies, waits for them, and re-layouts  1.57 us (5%)
  between operations  0.66 us (2%)
    pallas_call x1, Pallas kernels, shards(): pl.pallas_call(functools.partial(kernel, grps, n), out_shape=jax.ShapeDty...  30 us
    unnamed x1, local copies, waits for them, and re-layouts  1.57 us

commit v1 on v0

--- a/solution.py
+++ b/solution.py
@@ -23,7 +23,7 @@
     return jax.nn.gelu(value).astype(BF16)
 
 
-def kernel(grps, n, feat_any, live, neigh, w1_any, w2_any, wm_any, wc_any, wp_any, wo_any, out, levels, mats, sems):
+def kernel(grps, n, feat_any, live_any, neigh_any, w1_any, w2_any, wm_any, wc_any, wp_any, wo_any, out, levels, mats, live, neigh, sems):
     g, m = lax.axis_index("grp"), lax.axis_index("ch")
     q = n // 2
     half, tile = m // q, m % q
@@ -54,7 +54,7 @@
     loads = [
         pltpu.make_async_copy(source, target, local_sem.at[i])
         for i, (source, target) in enumerate(
-            [(w1_any, w1), (w2_any, w2), (wm_any, wm), (wo_any, wo), (wc_any, wc.at[m]), (wp_any, wp.at[m]), (feat_any, feat)]
+            [(w1_any, w1), (w2_any, w2), (wm_any, wm), (wo_any, wo), (wc_any, wc.at[m]), (wp_any, wp.at[m]), (live_any, live), (neigh_any, neigh), (feat_any, feat)]
         )
     ]
     for load in loads[-1:] + loads[:-1]:
@@ -253,18 +253,19 @@
     for r in range(1, n):
         project_copy(r, m).start()
     receive(leaf_a)
-    send_weights(1)
+    loads[6].wait()
+    loads[7].wait()
     extend(leaf_a)
     first = convolve_leaf(leaf_a, b1)
 
     leaf_b["v"][...] = first.astype(F32).reshape(edge, edge, edge, slots * c0)
     caps_of(leaf_b)
     send(leaf_b)
+    send_weights(1)
     loads[1].wait()
     fill_diagonal(w2, b2)
     hand_on(0)
     receive(leaf_b)
-    send_weights(2)
     extend(leaf_b)
     second = convolve_leaf(leaf_b, b2)
 
@@ -284,6 +285,7 @@
             mid["v"][x, y] = pooled[at : at + side]
     caps_of(mid)
     send(mid)
+    send_weights(2)
     loads[2].wait()
     fill_upright(wm, bm)
     hand_on(1)
@@ -415,7 +417,7 @@
         pltpu.VMEM((slots * small**3, taps * c1), F32),
     ]
     sems = [
-        pltpu.SemaphoreType.DMA((7,)),
+        pltpu.SemaphoreType.DMA((9,)),
         pltpu.SemaphoreType.DMA((PIECES, n - 1)),
         pltpu.SemaphoreType.DMA((PIECES, n - 1)),
         pltpu.SemaphoreType.DMA((n - 1,)),
@@ -426,10 +428,10 @@
     stay = pl.BlockSpec(memory_space=pl.ANY)
     return pl.pallas_call(
         functools.partial(kernel, grps, n),
-        out_shape=jax.ShapeDtypeStruct(features.shape, BF16),
-        in_specs=[stay, smem, smem] + [stay] * 6,
+        out_shape=pltpu.VMEM(features.shape, BF16),
+        in_specs=[stay] * 9,
         out_specs=vmem,
-        scratch_shapes=[levels, mats, sems],
+        scratch_shapes=[levels, mats, pltpu.SMEM(live_counts.shape, jnp.int32), pltpu.SMEM(neighbours.shape, jnp.int32), sems],
         compiler_params=pltpu.CompilerParams(collective_id=0, has_side_effects=True),
     )(features, live_counts, neighbours, w_first, w_second, w_middle, w_coarse, w_project, w_output)
 

time: 32.5 us -> 29.3 us (0.902)
  Pallas kernels: 30 us -> 27.7 us
  local copies, waits for them, and re-layouts: 1.57 us -> 0.66 us
    pallas_call x1, Pallas kernels: 30 us -> 27.7 us  [shards(): pl.pallas_call(functools.partial(kernel, grps, n), out_shape=pltpu.VMEM(f...]
    unnamed x1, local copies, waits for them, and re-layouts: 1.57 us -> 0.66 us
where the time goes in v1:
time: 29.3 us; the launch traced here: 29 us
  Pallas kernels  27.7 us (95%)
  local copies, waits for them, and re-layouts  0.66 us (2%)
  between operations  0.66 us (2%)
    pallas_call x1, Pallas kernels, shards(): pl.pallas_call(functools.partial(kernel, grps, n), out_shape=pltpu.VMEM(f...  27.7 us
    unnamed x1, local copies, waits for them, and re-layouts  0.66 us

profile of v1, /device:TPU:0, one launch (start us, length us, event | category | flops | bytes accessed | tf_op | source)
XLA Modules:
  0.0 29.0 jit_solution(17424306306225828888)
XLA Ops:
  0.7 27.7 %shard_map.91 = bf16[2,64,512]{2,1,0:T(8,128)(2,1)S(1)} custom-call(bf16[2,64,512]{2,1,0:T(8,128)(2,1)} %feat_any.1, s32[1]{0:T(128)S(6)} %copy.12.live_any, s32[2,27]{1,0:T(2,128)} %neigh_any.1, bf16[27,64,64]{2,1,0:T(8,128)(2,1)} %w1_any.1, bf16[27,64,64]{2,1,0:T(8,128)(2,1)} %w2_any.1, bf16[27,64,128]{2,1,0:T(8,128)(2,1)} %bitcast.1, ...), custom_call_target="tpu_custom_call" | custom-call | tf_op jit(solution)/shard_map/pallas_call | solution.py:429
  28.4 0.7 %copy.11 = bf16[2,64,512]{2,1,0:T(8,128)(2,1)} copy(bf16[2,64,512]{2,1,0:T(8,128)(2,1)S(1)} %shard_map.91) | data formatting | bytes 262144

commit v2 on v1

--- a/solution.py
+++ b/solution.py
@@ -1,4 +1,6 @@
 import functools
+
+import numpy as np
 
 import jax
 import jax.numpy as jnp
@@ -23,44 +25,83 @@
     return jax.nn.gelu(value).astype(BF16)
 
 
-def kernel(grps, n, feat_any, live_any, neigh_any, w1_any, w2_any, wm_any, wc_any, wp_any, wo_any, out, levels, mats, live, neigh, sems):
+def kernel(grps, n, feat_any, live_any, neigh_any, w1_any, w2_any, wm_any, wc_any, wp_any, wo_any, table_any, out, levels, mats, live, neigh, sems):
     g, m = lax.axis_index("grp"), lax.axis_index("ch")
     q = n // 2
-    half, tile = m // q, m % q
+    half, place_y = m // q, m % q
     slots, c0, voxels = feat_any.shape
     edge = round(voxels ** (1 / 3))
     c1 = wm_any.shape[2]
 
     def has(partner):
         _, y, z = partner
-        return (tile + y >= 0) & (tile + y < q) & (g + z >= 0) & (g + z < grps)
+        return (place_y + y >= 0) & (place_y + y < q) & (g + z >= 0) & (g + z < grps)
 
     def coords(partner):
         h, y, z = partner
-        return g + z, ((1 - half) if h else half) * q + tile + y
+        return g + z, ((1 - half) if h else half) * q + place_y + y
 
     barrier = pltpu.get_barrier_semaphore()
-    for r in range(1, n):
-        pl.semaphore_signal(barrier, inc=1, device_id=(g, (m + r) % n), device_id_type=MESH)
     far = [p for p in PARTNERS if p[2] != 0]
-    for p in far:
+    for p in sorted(far, key=lambda p: -sum(abs(s) for s in p)):
 
         @pl.when(has(p))
         def _():
             pl.semaphore_signal(barrier, inc=1, device_id=coords(p), device_id_type=MESH)
 
-    (feat, w1, w2, wm, wo, wc, wp, b1, b2, bm, im_leaf, im_mid, im_coarse) = mats
-    (local_sem, wsend, wrecv, psend, precv) = sems
+    for r in range(1, n):
+        pl.semaphore_signal(barrier, inc=1, device_id=(g, (m + r) % n), device_id_type=MESH)
+
+    (feat, w1, w2, wm, wo, wc, wp, b1, b2, f1, f2, bm, im_leaf, im_mid, table, gather, ext_leaf, planes, acc) = mats
+    (local_sem, wsend, wrecv, hsend, hrecv) = sems
+    for i, level in enumerate(levels):
+        level.update(send=hsend.at[i % 2], recv=hrecv.at[i % 2])
     loads = [
         pltpu.make_async_copy(source, target, local_sem.at[i])
         for i, (source, target) in enumerate(
-            [(w1_any, w1), (w2_any, w2), (wm_any, wm), (wo_any, wo), (wc_any, wc.at[m]), (wp_any, wp.at[m]), (live_any, live), (neigh_any, neigh), (feat_any, feat)]
+            [(w1_any, w1), (w2_any, w2), (wm_any, wm), (wo_any, wo), (wc_any, wc.at[m, pl.ds(0, wc_any.shape[0])]), (wp_any, wp), (live_any, live), (neigh_any, neigh), (table_any, table), (feat_any, feat)]
         )
     ]
     for load in loads[-1:] + loads[:-1]:
         load.start()
 
+    tile = 2 * edge
+    area = edge * edge
+
+    def leaf_piece(level, partner):
+        h, y, z = partner
+        upper, right = (1 if z > 0 else 0), (1 if y > 0 else 0)
+        far_side = 1 - half
+        if z:
+            if y:
+                return level["send_l"].at[upper, right]
+            if h:
+                return level["send_z"].at[upper, pl.ds(pl.multiple_of(far_side * (area - tile), tile), tile)]
+            return level["send_z"].at[upper]
+        if not h:
+            return level["send_y"].at[right]
+        start, size = far_side * (edge - 1) * area + right * (area - tile if y else 0), tile if y else area
+        return level["flat"].at[pl.ds(pl.multiple_of(start, tile), size)]
+
+    def unpack(level, partner):
+        h, y, z = partner
+        index = PARTNERS.index(partner)
+        value = level["land"][index][...].astype(F32)
+        target = level["got"][index]
+        if value.shape[0] > tile:
+            target[...] = value.reshape(target.shape)
+        elif y and z:
+            target[...] = value[:edge]
+        elif y:
+            target[0] = value[edge:] if y < 0 else value[:edge]
+        else:
+            target[...] = jnp.where(half == 0, value[:edge], value[edge:])
+
     def piece_of(level, partner):
+        if "lines" in level:
+            return leaf_piece(level, partner)
+        if "rows" in level:
+            return level["rows"]
         h, y, z = partner
         volume, caps = level["v"], level["caps"]
         length = volume.shape[0]
@@ -75,7 +116,7 @@
         back = PARTNERS.index((h, -y, -z))
         return pltpu.make_async_remote_copy(
             src_ref=piece_of(level, PARTNERS[index]),
-            dst_ref=level["got"][back],
+            dst_ref=level["got"].at[back] if "rows" in level else level.get("land", level["got"])[back],
             send_sem=level["send"].at[index],
             recv_sem=level["recv"].at[back],
             device_id=coords(PARTNERS[index]),
@@ -96,6 +137,22 @@
             @pl.when(has(PARTNERS[i]))
             def _():
                 copy_to(level, i).start()
+
+    order_of = [PARTNERS[i] for i in order]
+
+    def sent(level):
+        for i in order:
+
+            @pl.when(has(PARTNERS[i]))
+            def _():
+                copy_to(level, i).wait_send()
+
+    def wait_for(level, partners):
+        for h, y, z in partners:
+
+            @pl.when(has((h, -y, -z)))
+            def _():
+                copy_to(level, PARTNERS.index((h, y, z))).wait_recv()
 
     def receive(level):
         for i in order:
@@ -153,14 +210,204 @@
                         )
             ext[target_at(x), target_at(y), target_at(z), :] = value
 
-    taps = wc.shape[1]
+    half_lanes = slots * c0 // 2
+    lane = lax.broadcasted_iota(jnp.int32, (edge, slots * c0), 1)
+    block_of = (lane >= half_lanes).astype(jnp.int32)
+    first_of = {}
+    for p in [(0, 0, 0)] + PARTNERS:
+        a, b = coords(p)
+        first_of[p] = jnp.where(has(p), (a * n + b) * 2, -8)
+
+    def choose(column, rows, sources):
+        wanted = jnp.where(block_of == 1, neigh[1, column], neigh[0, column])
+        owner = block_of
+        if rows < edge:
+            wanted, owner = wanted[:rows], owner[:rows]
+        value = None
+        for p, found in sources:
+            pieces = [found[r : r + min(rows, edge)] for r in range(0, rows, edge)]
+            straight, crossed = wanted == first_of[p] + owner, wanted == first_of[p] + 1 - owner
+            old = value if value is not None else [jnp.zeros_like(piece) for piece in pieces]
+            value = [
+                jnp.where(straight, piece, jnp.where(crossed, pltpu.roll(piece, half_lanes, 1), before))
+                for piece, before in zip(pieces, old)
+            ]
+        return value
+
+    def put(plane, kind, value):
+        if kind == "face":
+            for r, rows in enumerate(value):
+                at = (r + 1) * 2 * edge + 1
+                planes[plane, at : at + edge, :] = rows
+            return
+        axis, place = kind
+        if axis == "row":
+            at = place * 2 * edge + 1
+            planes[plane, at : at + edge, :] = value[0]
+        elif axis == "column":
+            planes[plane, pl.ds(2 * edge + place, edge, stride=2 * edge), :] = value[0]
+        else:
+            at = place[0] * 2 * edge + place[1]
+            planes[plane, at : at + 1, :] = value[0]
+
+    def add_plane(plane, weights, where):
+        parts = []
+        for i in range(3):
+            for j in range(3):
+                rows = [planes[plane, (r + i) * 2 * edge + j : (r + i) * 2 * edge + j + edge, :] for r in range(edge)]
+                parts.append(jnp.concatenate(rows, axis=0).astype(BF16))
+        update = matmul_nt(jnp.concatenate(parts, axis=1), weights)
+        axis, at = where
+        if axis == "x":
+            acc[pl.ds(at, area), :] += update
+            return
+        for r in range(edge):
+            rows = update[r * edge : (r + 1) * edge]
+            if axis == "y":
+                acc[r * area + at : r * area + at + edge, :] += rows
+            else:
+                acc[pl.ds(r * area + at, edge, stride=edge), :] += rows
+
+    small = edge // 4
+    cells = small**3
+
+    def fill_gather():
+        sub = lax.broadcasted_iota(jnp.int32, (8, gather.shape[1] // 3), 0)
+        col = lax.broadcasted_iota(jnp.int32, (8, gather.shape[1] // 3), 1)
+        width = sub.shape[1]
+        entries = [neigh[b, d] * cells for b in range(slots) for d in range(27)] + list(range(cells))
+        blocks = []
+        for start in range(0, width, 8):
+            block = jnp.zeros(sub.shape, jnp.int32)
+            for s, entry in enumerate(entries[start : start + 8]):
+                block = jnp.where(sub == s, entry, block)
+            blocks.append(block.astype(F32))
+        keys = jnp.dot(table[...], jnp.concatenate(blocks, axis=0).astype(BF16), preferred_element_type=F32)
+        rows = slots * cells
+        for k in range(3):
+            offer = jnp.full(sub.shape, -1000, jnp.int32)
+            for i, p in enumerate([(0, 0, 0)] + PARTNERS):
+                at = i * rows - k * width
+                offer = jnp.where((col >= at) & (col < at + rows), first_of[p] * cells + col - at, offer)
+            offer = jnp.broadcast_to(offer[:1].astype(F32), keys.shape)
+            gather[:, k * width : (k + 1) * width] = jnp.where(keys == offer, 1.0, 0.0).astype(BF16)
+
+    def column_of(x, y, z):
+        return 9 * (x + 1) + 3 * (y + 1) + z + 1
+
+    def halo(level, weights, faces):
+        volume, caps, lines = level["v"], level["caps"], level["lines"]
+        got = {p: level["got"][i] for i, p in enumerate(PARTNERS)}
+        last = edge - 1
+        near = lambda s: 0 if s > 0 else last
+        beyond = lambda s: 0 if s < 0 else edge + 1
+        flag = lambda s: 0 if s > 0 else 1
+        line_y = lambda y: slice(near(y) * edge, near(y) * edge + edge)
+        skip = lambda start: pl.ds(start, edge, stride=edge)
+
+        def arrive(partners):
+            wait_for(level, partners)
+            for p in partners:
+                unpack(level, p)
+
+        arrive([(0, 0, -1), (0, 0, 1)])
+        for z in (-1, 1):
+            plane = 4 + (z > 0)
+            sources = [((0, 0, 0), caps[flag(z)]), ((0, 0, z), got[0, 0, z][...])]
+            put(plane, "face", choose(column_of(0, 0, z), edge * edge, sources))
+            add_plane(plane, faces[plane - 2], ("z", last - near(z)))
+        arrive([(0, -1, 0), (0, 1, 0)] + [(0, y, z) for y in (-1, 1) for z in (-1, 1)])
+        for y in (-1, 1):
+            plane = 2 + (y > 0)
+            flat = got[0, y, 0].reshape(edge * edge, slots * c0)
+            own = volume[:, line_y(y), :].reshape(edge * edge, slots * c0)
+            sources = [((0, 0, 0), own), ((0, y, 0), flat[...])]
+            put(plane, "face", choose(column_of(0, y, 0), edge * edge, sources))
+            for z in (-1, 1):
+                sources = [
+                    ((0, 0, 0), lines[flag(z), flag(y)]),
+                    ((0, y, 0), flat[skip(near(z)), :]),
+                    ((0, 0, z), got[0, 0, z][skip(near(y)), :]),
+                    ((0, y, z), got[0, y, z][...]),
+                ]
+                put(plane, ("column", beyond(z)), choose(column_of(0, y, z), edge, sources))
+            add_plane(plane, faces[plane - 2], ("y", (last - near(y)) * edge))
+        for x in (-1, 1):
+            plane, xe = (x > 0) + 0, near(x)
+            put(plane, "face", choose(column_of(x, 0, 0), edge * edge, [((0, 0, 0), volume[xe])]))
+            for y in (-1, 1):
+                sources = [((0, 0, 0), volume[xe, line_y(y), :]), ((0, y, 0), got[0, y, 0][xe])]
+                put(plane, ("row", beyond(y)), choose(column_of(x, y, 0), edge, sources))
+            for z in (-1, 1):
+                span = slice(xe * edge, xe * edge + edge)
+                sources = [((0, 0, 0), caps[flag(z), span, :]), ((0, 0, z), got[0, 0, z][span, :])]
+                put(plane, ("column", beyond(z)), choose(column_of(x, 0, z), edge, sources))
+            for y in (-1, 1):
+                for z in (-1, 1):
+                    at = xe * edge + near(y)
+                    sources = [
+                        ((0, 0, 0), lines[flag(z), flag(y), xe : xe + 1, :]),
+                        ((0, y, 0), got[0, y, 0][xe, near(z) : near(z) + 1, :]),
+                        ((0, 0, z), got[0, 0, z][at : at + 1, :]),
+                        ((0, y, z), got[0, y, z][xe : xe + 1, :]),
+                    ]
+                    put(plane, ("cell", (beyond(y), beyond(z))), choose(column_of(x, y, z), 1, sources))
+            add_plane(plane, weights[2 * (x > 0)], ("x", (last - xe) * edge * edge))
+        arrive([p for p in order_of[::-1] if p[0] == 1])
+        plane = 6
+        x = 1 - 2 * half
+        face = got[1, 0, 0]
+        put(plane, "face", choose(column_of(x, 0, 0), edge * edge, [((1, 0, 0), face[0])]))
+        for y in (-1, 1):
+            sources = [((1, 0, 0), face[0, line_y(y), :]), ((1, y, 0), got[1, y, 0][0])]
+            put(plane, ("row", beyond(y)), choose(column_of(x, y, 0), edge, sources))
+        for z in (-1, 1):
+            sources = [((1, 0, 0), face[0, skip(near(z)), :]), ((1, 0, z), got[1, 0, z][...])]
+            put(plane, ("column", beyond(z)), choose(column_of(x, 0, z), edge, sources))
+        for y in (-1, 1):
+            for z in (-1, 1):
+                at = near(y) * edge + near(z)
+                sources = [
+                    ((1, 0, 0), face[0, at : at + 1, :]),
+                    ((1, y, 0), got[1, y, 0][0, near(z) : near(z) + 1, :]),
+                    ((1, 0, z), got[1, 0, z][near(y) : near(y) + 1, :]),
+                    ((1, y, z), got[1, y, z][pl.ds(half * last, 1), :]),
+                ]
+                put(plane, ("cell", (beyond(y), beyond(z))), choose(column_of(x, y, z), 1, sources))
+        facing = pl.multiple_of((1 - half) * last * edge * edge, edge * edge)
+        add_plane(plane, weights[2 * (1 - half)], ("x", facing))
+
+    def surface(level):
+        volume, caps, lines = level["v"], level["caps"], level["lines"]
+        for k, z in enumerate((0, edge - 1)):
+            for x in range(edge):
+                caps[k, x * edge : (x + 1) * edge, :] = volume[x, pl.ds(z, edge, stride=edge), :]
+            for j, y in enumerate((0, edge - 1)):
+                line = caps[k, pl.ds(y, edge, stride=edge), :]
+                lines[k, j] = line
+                level["send_l"][k, j] = jnp.concatenate([line, line], axis=0).astype(BF16)
+            level["send_z"][k] = caps[k].astype(BF16)
+        for j, y in enumerate((0, edge - 1)):
+            face = volume[:, y * edge : (y + 1) * edge, :].reshape(area, slots * c0)
+            level["send_y"][j] = face.astype(BF16)
+
+    def fill_faces(weights, target):
+        width = slots * c0
+        for k in range(2):
+            for i in range(3):
+                target[k, :, 3 * i * width : 3 * (i + 1) * width] = weights[i, :, 6 * k * width : (6 * k + 3) * width]
+                for j in range(3):
+                    at, tap = (3 * i + j) * width, (3 * j + 2 * k) * width
+                    target[2 + k, :, at : at + width] = weights[i, :, tap : tap + width]
+
+    taps = wc.shape[1] - 1
 
     pairs = n // 2
     pair, core = m // 2, m % 2
     partner = pair * 2 + 1 - core
 
     def weight_copies(part, role, r):
-        first, last = taps * part // PIECES, taps * (part + 1) // PIECES
+        first, last = (taps + 1) * part // PIECES, (taps + 1) * (part + 1) // PIECES
         other = (pair + pairs - r) % pairs * 2
         owner, came = [(m, partner), (m, other + core), (other + core, other + 1 - core)][role]
         target = (pair + r) % pairs * 2 + core if role == 1 else partner
@@ -179,16 +426,6 @@
 
         return functools.partial(copy, owner), functools.partial(copy, came)
 
-    def project_copy(r, other):
-        return pltpu.make_async_remote_copy(
-            src_ref=wp.at[other],
-            dst_ref=wp.at[other],
-            send_sem=psend.at[r - 1],
-            recv_sem=precv.at[r - 1],
-            device_id=(g, (m + r) % n),
-            device_id_type=MESH,
-        )
-
     def send_weights(part):
         for r in range(1, pairs):
             weight_copies(part, 1, r)[0]().start()
@@ -221,53 +458,64 @@
                     there = weights[t] if other == b else empty
                     target[t // 9, at : at + rows, other * width : (other + 1) * width] = there
 
-    def convolve_leaf(level, weights):
-        ext, length, lanes = level["ext"], edge, level["v"].shape[3]
+    def convolve_own(level, weights):
+        lanes = slots * c0
+        inside = slice(1, edge + 1)
+        ext_leaf[inside, inside, inside, :] = level["v"][...].reshape(edge, edge, edge, lanes)
         for k in range(9):
             y, z = k // 3, k % 3
-            rows = ext[:, y : y + length, z : z + length, :].reshape(length + 2, length * length, lanes)
+            rows = ext_leaf[:, y : y + edge, z : z + edge, :].reshape(edge + 2, edge * edge, lanes)
             im_leaf[:, :, k * lanes : (k + 1) * lanes] = rows.astype(BF16)
         total = None
         for x in range(3):
-            window = im_leaf[x : x + length].reshape(length**3, 9 * lanes)
+            window = im_leaf[x : x + edge].reshape(edge**3, 9 * lanes)
             term = matmul_nt(window, weights[x])
             total = term if total is None else total + term
-        return rounded_gelu(total)
+        acc[...] = total
 
     leaf_a, leaf_b, mid, low = levels
     loads[-1].wait()
     packed = feat[...].reshape(slots * c0, voxels).astype(F32)
-    leaf_a["v"][...] = packed.T.reshape(edge, edge, edge, slots * c0)
-    caps_of(leaf_a)
+    turned = packed.T
+    leaf_a["v"][...] = turned.reshape(edge, area, slots * c0)
+    leaf_a["flat"][...] = turned.astype(BF16)
+    surface(leaf_a)
+    ext_leaf[...] = jnp.zeros_like(ext_leaf)
+    planes[...] = jnp.zeros_like(planes)
     peers = n - 1
     for p in far:
         peers = peers + has(p).astype(jnp.int32)
     pl.semaphore_wait(barrier, peers)
 
     send(leaf_a)
+    loads[4].wait()
+    loads[5].wait()
+    wc[m, taps] = jnp.concatenate([wp[...]] * (c1 // c0), axis=1)
+    send_weights(0)
     loads[0].wait()
     fill_diagonal(w1, b1)
-    loads[4].wait()
-    loads[5].wait()
-    send_weights(0)
-    for r in range(1, n):
-        project_copy(r, m).start()
-    receive(leaf_a)
+    fill_faces(b1, f1)
+    convolve_own(leaf_a, b1)
     loads[6].wait()
     loads[7].wait()
-    extend(leaf_a)
-    first = convolve_leaf(leaf_a, b1)
-
-    leaf_b["v"][...] = first.astype(F32).reshape(edge, edge, edge, slots * c0)
-    caps_of(leaf_b)
+    loads[8].wait()
+    fill_gather()
+    halo(leaf_a, b1, f1)
+    first = rounded_gelu(acc[...])
+
+    leaf_b["flat"][...] = first
+    leaf_b["v"][...] = first.astype(F32).reshape(edge, area, slots * c0)
+    surface(leaf_b)
     send(leaf_b)
     send_weights(1)
     loads[1].wait()
     fill_diagonal(w2, b2)
+    fill_faces(b2, f2)
+    convolve_own(leaf_b, b2)
     hand_on(0)
-    receive(leaf_b)
-    extend(leaf_b)
-    second = convolve_leaf(leaf_b, b2)
+    sent(leaf_a)
+    halo(leaf_b, b2, f2)
+    second = rounded_gelu(acc[...])
 
     def halving(length):
         small = length // 2
@@ -289,6 +537,7 @@
     loads[2].wait()
     fill_upright(wm, bm)
     hand_on(1)
+    sent(leaf_b)
     receive(mid)
     extend(mid)
     lanes = slots * c0
@@ -303,13 +552,9 @@
         total = term if total is None else total + term
     middle = rounded_gelu(total)
 
-    small = side // 2
-    pooled = jnp.dot(halving(side), middle, preferred_element_type=F32).astype(BF16).astype(F32)
-    for x in range(small):
-        for y in range(small):
-            at = (x * small + y) * small
-            low["v"][x, y] = pooled[at : at + small]
-    caps_of(low)
+    pooled = jnp.dot(halving(side), middle, preferred_element_type=F32)
+    pooled = jnp.concatenate([pooled[:, b * c1 : (b + 1) * c1] for b in range(slots)], axis=0).astype(BF16)
+    low["rows"][...] = pooled
     send(low)
     loads[3].wait()
     skip_top, skip_bottom = diagonal(wo[:, :c0])
@@ -322,27 +567,20 @@
         weight_copies(part, 0, 0)[1]().wait_recv()
         for r in range(1, pairs):
             weight_copies(part, 2, r)[1]().wait_recv()
-    for r in range(1, n):
-        project_copy(r, (m + n - r) % n).wait_recv()
     receive(low)
-    extend(low)
-    cells = small**3
-    for t in range(taps):
-        tx, ty, tz = t // 9, t // 3 % 3, t % 3
-        for b in range(slots):
-            for x in range(small):
-                for y in range(small):
-                    at = b * cells + (x * small + y) * small
-                    im_coarse[at : at + small, t * c1 : (t + 1) * c1] = low["ext"][
-                        x + tx, y + ty, tz : tz + small, b * c1 : (b + 1) * c1
-                    ]
-    total = None
+    sources = [pooled]
+    for i, p in enumerate(PARTNERS):
+        sources.append(jnp.where(has(p), low["got"][i], jnp.zeros_like(pooled)))
+    spare = gather.shape[1] - len(sources) * slots * cells
+    sources.append(jnp.zeros((spare, c1), BF16))
+    spread = jnp.dot(gather[...], jnp.concatenate(sources, axis=0), preferred_element_type=F32).astype(BF16)
+    rows = slots * cells
+    window = jnp.concatenate([spread[t * rows : (t + 1) * rows] for t in range(taps)], axis=1)
     c2 = n * wc.shape[2]
-    for t in range(taps):
-        term = matmul_nt(im_coarse[:, t * c1 : (t + 1) * c1].astype(BF16), wc[:, t].reshape(c2, c1))
-        total = term if total is None else total + term
+    weights = jnp.concatenate([wc[:, t].reshape(c2, c1) for t in range(taps)], axis=1)
+    total = matmul_nt(window, weights)
     hidden = rounded_gelu(total)
-    coarse = jnp.dot(hidden, wp[...].reshape(c2, c0), preferred_element_type=F32)
+    coarse = jnp.dot(hidden, wc[:, taps].reshape(c2, c1)[:, :c0], preferred_element_type=F32)
     coarse = jnp.concatenate([coarse[b * cells : (b + 1) * cells] for b in range(slots)], axis=1).astype(BF16)
     row = lax.broadcasted_iota(jnp.int32, (voxels, cells), 0)
     column = lax.broadcasted_iota(jnp.int32, (voxels, cells), 1)
@@ -357,15 +595,8 @@
     for b in range(slots):
         out[b] = mixed[b * c0 : (b + 1) * c0]
 
-    for level in levels:
-        for i in order:
-
-            @pl.when(has(PARTNERS[i]))
-            def _():
-                copy_to(level, i).wait_send()
-
-    for r in range(1, n):
-        project_copy(r, m).wait_send()
+    sent(mid)
+    sent(low)
     for part in range(PIECES):
         weight_copies(part, 0, 0)[0]().wait_send()
         for r in range(1, pairs):
@@ -373,6 +604,42 @@
             weight_copies(part, 2, r)[0]().wait_send()
 
 
+def leaf_scratch(length, lanes):
+    def got(partner):
+        h, y, z = partner
+        if z == 0:
+            return pltpu.VMEM((1 if h else length, length if y else length**2, lanes), F32)
+        return pltpu.VMEM((length if h or y else length**2, lanes), F32)
+
+    return dict(
+        v=pltpu.VMEM((length, length**2, lanes), F32),
+        caps=pltpu.VMEM((2, length**2, lanes), F32),
+        lines=pltpu.VMEM((2, 2, length, lanes), F32),
+        flat=pltpu.VMEM((length**3, lanes), BF16),
+        send_y=pltpu.VMEM((2, length**2, lanes), BF16),
+        send_z=pltpu.VMEM((2, length**2, lanes), BF16),
+        send_l=pltpu.VMEM((2, 2, 2 * length, lanes), BF16),
+        land=[pltpu.VMEM((length**2 if sum(map(abs, p)) == 1 else 2 * length, lanes), BF16) for p in PARTNERS],
+        got=[got(p) for p in PARTNERS],
+    )
+
+
+def coarse_table(slots, small):
+    cells = small**3
+    table = np.zeros((len(OFFSETS) * slots * cells, 128), np.float32)
+    row = 0
+    for tap in OFFSETS:
+        for b in range(slots):
+            for cell in np.ndindex(small, small, small):
+                there = np.array(cell) + np.array(tap)
+                x, y, z = there // small + 1
+                table[row, b * 27 + 9 * x + 3 * y + z] = 1
+                x, y, z = there % small
+                table[row, slots * 27 + (x * small + y) * small + z] = 1
+                row += 1
+    return jnp.asarray(table, BF16)
+
+
 def level_scratch(length, lanes):
     def got(partner):
         h, y, z = partner
@@ -383,8 +650,6 @@
         caps=pltpu.VMEM((2, length, length, 1, lanes), F32),
         ext=pltpu.VMEM((length + 2,) * 3 + (lanes,), F32),
         got=[got(p) for p in PARTNERS],
-        send=pltpu.SemaphoreType.DMA((len(PARTNERS),)),
-        recv=pltpu.SemaphoreType.DMA((len(PARTNERS),)),
     )
 
 
@@ -396,32 +661,42 @@
     lanes = slots * c0
     side, small = edge // 2, edge // 4
     levels = [
-        level_scratch(edge, lanes),
-        level_scratch(edge, lanes),
+        leaf_scratch(edge, lanes),
+        leaf_scratch(edge, lanes),
         level_scratch(side, lanes),
-        level_scratch(small, slots * c1),
+        dict(
+            rows=pltpu.VMEM((slots * small**3, c1), BF16),
+            got=pltpu.VMEM((len(PARTNERS), slots * small**3, c1), BF16),
+        ),
     ]
+    table = coarse_table(slots, small)
     mats = [
         pltpu.VMEM(features.shape, BF16),
         pltpu.VMEM(w_first.shape, BF16),
         pltpu.VMEM(w_second.shape, BF16),
         pltpu.VMEM(w_middle.shape, BF16),
         pltpu.VMEM(w_output.shape, BF16),
-        pltpu.VMEM((n,) + w_coarse.shape, BF16),
-        pltpu.VMEM((n,) + w_project.shape, BF16),
+        pltpu.VMEM((n, taps + 1) + w_coarse.shape[1:], BF16),
+        pltpu.VMEM(w_project.shape, BF16),
         pltpu.VMEM((3, lanes, 9 * lanes), BF16),
         pltpu.VMEM((3, lanes, 9 * lanes), BF16),
+        pltpu.VMEM((4, lanes, 9 * lanes), BF16),
+        pltpu.VMEM((4, lanes, 9 * lanes), BF16),
         pltpu.VMEM((3, 9 * lanes, slots * c1), BF16),
         pltpu.VMEM((edge + 2, edge * edge, 9 * lanes), BF16),
         pltpu.VMEM((side + 2, side * side, 9 * lanes), F32),
-        pltpu.VMEM((slots * small**3, taps * c1), F32),
+        pltpu.VMEM(table.shape, BF16),
+        pltpu.VMEM((table.shape[0], 3 * 128), BF16),
+        pltpu.VMEM((edge + 2,) * 3 + (lanes,), F32),
+        pltpu.VMEM((7, (edge + 2) * 2 * edge, lanes), F32),
+        pltpu.VMEM((edge**3, lanes), F32),
     ]
     sems = [
-        pltpu.SemaphoreType.DMA((9,)),
+        pltpu.SemaphoreType.DMA((10,)),
         pltpu.SemaphoreType.DMA((PIECES, n - 1)),
         pltpu.SemaphoreType.DMA((PIECES, n - 1)),
-        pltpu.SemaphoreType.DMA((n - 1,)),
-        pltpu.SemaphoreType.DMA((n - 1,)),
+        pltpu.SemaphoreType.DMA((2, len(PARTNERS))),
+        pltpu.SemaphoreType.DMA((2, len(PARTNERS))),
     ]
     smem = pl.BlockSpec(memory_space=pltpu.SMEM)
     vmem = pl.BlockSpec(memory_space=pltpu.VMEM)
@@ -429,11 +704,11 @@
     return pl.pallas_call(
         functools.partial(kernel, grps, n),
         out_shape=pltpu.VMEM(features.shape, BF16),
-        in_specs=[stay] * 9,
+        in_specs=[stay] * 10,
         out_specs=vmem,
         scratch_shapes=[levels, mats, pltpu.SMEM(live_counts.shape, jnp.int32), pltpu.SMEM(neighbours.shape, jnp.int32), sems],
         compiler_params=pltpu.CompilerParams(collective_id=0, has_side_effects=True),
-    )(features, live_counts, neighbours, w_first, w_second, w_middle, w_coarse, w_project, w_output)
+    )(features, live_counts, neighbours, w_first, w_second, w_middle, w_coarse, w_project, w_output, table)
 
 
 def solution(mesh):

time: 29.3 us -> 26.3 us (0.90)
  Pallas kernels: 27.7 us -> 24.8 us
    pallas_call x1, Pallas kernels: 27.7 us -> 24.8 us  [shards(): pl.pallas_call(functools.partial(kernel, grps, n), out_shape=pltpu.VMEM(f...]
where the time goes in v2:
time: 26.3 us; the launch traced here: 26.2 us
  Pallas kernels  24.8 us (94%)
  local copies, waits for them, and re-layouts  0.66 us (3%)
  between operations  0.66 us (3%)
    pallas_call x1, Pallas kernels, shards(): pl.pallas_call(functools.partial(kernel, grps, n), out_shape=pltpu.VMEM(f...  24.8 us
    unnamed x1, local copies, waits for them, and re-layouts  0.66 us

profile of v2, /device:TPU:0, one launch (start us, length us, event | category | flops | bytes accessed | tf_op | source)
XLA Modules:
  0.0 26.2 jit_solution(6568179370352725695)
XLA Ops:
  0.7 24.8 %shard_map.100 = bf16[2,64,512]{2,1,0:T(8,128)(2,1)S(1)} custom-call(bf16[2,64,512]{2,1,0:T(8,128)(2,1)} %feat_any.1, s32[1]{0:T(128)S(6)} %copy.13.live_any, s32[2,27]{1,0:T(2,128)} %neigh_any.1, bf16[27,64,64]{2,1,0:T(8,128)(2,1)} %w1_any.1, bf16[27,64,64]{2,1,0:T(8,128)(2,1)} %w2_any.1, bf16[27,64,128]{2,1,0:T(8,128)(2,1)} %bitcast.1, ...), custom_call_target="tpu_custom_call" | custom-call | tf_op jit(solution)/shard_map/pallas_call | solution.py:704
  25.5 0.7 %copy.12 = bf16[2,64,512]{2,1,0:T(8,128)(2,1)} copy(bf16[2,64,512]{2,1,0:T(8,128)(2,1)S(1)} %shard_map.100) | data formatting | bytes 262144

commit v3 on v2

--- a/solution.py
+++ b/solution.py
@@ -59,13 +59,12 @@
     loads = [
         pltpu.make_async_copy(source, target, local_sem.at[i])
         for i, (source, target) in enumerate(
-            [(w1_any, w1), (w2_any, w2), (wm_any, wm), (wo_any, wo), (wc_any, wc.at[m, pl.ds(0, wc_any.shape[0])]), (wp_any, wp), (live_any, live), (neigh_any, neigh), (table_any, table), (feat_any, feat)]
+            [(w1_any, w1), (w2_any, w2), (wm_any, wm), (wo_any, wo), (wc_any, wc.at[m % 2, m // 2, pl.ds(0, wc_any.shape[0])]), (wp_any, wp), (live_any, live), (neigh_any, neigh), (table_any, table), (feat_any, feat)]
         )
     ]
     for load in loads[-1:] + loads[:-1]:
         load.start()
 
-    tile = 2 * edge
     area = edge * edge
 
     def leaf_piece(level, partner):
@@ -76,26 +75,18 @@
             if y:
                 return level["send_l"].at[upper, right]
             if h:
-                return level["send_z"].at[upper, pl.ds(pl.multiple_of(far_side * (area - tile), tile), tile)]
+                return level["send_z"].at[upper, pl.ds(pl.multiple_of(far_side * (area - edge), edge), edge)]
             return level["send_z"].at[upper]
         if not h:
             return level["send_y"].at[right]
-        start, size = far_side * (edge - 1) * area + right * (area - tile if y else 0), tile if y else area
-        return level["flat"].at[pl.ds(pl.multiple_of(start, tile), size)]
+        start, size = far_side * (edge - 1) * area + right * (area - edge if y else 0), edge if y else area
+        return level["flat"].at[pl.ds(pl.multiple_of(start, edge), size)]
 
     def unpack(level, partner):
-        h, y, z = partner
         index = PARTNERS.index(partner)
         value = level["land"][index][...].astype(F32)
         target = level["got"][index]
-        if value.shape[0] > tile:
-            target[...] = value.reshape(target.shape)
-        elif y and z:
-            target[...] = value[:edge]
-        elif y:
-            target[0] = value[edge:] if y < 0 else value[:edge]
-        else:
-            target[...] = jnp.where(half == 0, value[:edge], value[edge:])
+        target[...] = value.reshape(target.shape)
 
     def piece_of(level, partner):
         if "lines" in level:
@@ -218,12 +209,11 @@
         a, b = coords(p)
         first_of[p] = jnp.where(has(p), (a * n + b) * 2, -8)
 
-    def choose(column, rows, sources):
+    def choose(column, rows, sources, value=None):
         wanted = jnp.where(block_of == 1, neigh[1, column], neigh[0, column])
         owner = block_of
         if rows < edge:
             wanted, owner = wanted[:rows], owner[:rows]
-        value = None
         for p, found in sources:
             pieces = [found[r : r + min(rows, edge)] for r in range(0, rows, edge)]
             straight, crossed = wanted == first_of[p] + owner, wanted == first_of[p] + 1 - owner
@@ -234,21 +224,22 @@
             ]
         return value
 
-    def put(plane, kind, value):
-        if kind == "face":
-            for r, rows in enumerate(value):
-                at = (r + 1) * 2 * edge + 1
-                planes[plane, at : at + edge, :] = rows
-            return
+    def spots(plane, kind):
         axis, place = kind
+        pitch = 2 * edge
+        if axis == "face":
+            return [(plane, slice((r + 1) * pitch + 1, (r + 1) * pitch + 1 + edge)) for r in range(edge)]
         if axis == "row":
-            at = place * 2 * edge + 1
-            planes[plane, at : at + edge, :] = value[0]
-        elif axis == "column":
-            planes[plane, pl.ds(2 * edge + place, edge, stride=2 * edge), :] = value[0]
-        else:
-            at = place[0] * 2 * edge + place[1]
-            planes[plane, at : at + 1, :] = value[0]
+            return [(plane, slice(place * pitch + 1, place * pitch + 1 + edge))]
+        if axis == "column":
+            return [(plane, pl.ds(pitch + place, edge, stride=pitch))]
+        return [(plane, slice(place[0] * pitch + place[1], place[0] * pitch + place[1] + 1))]
+
+    def put(plane, kind, column, rows, sources, add=False):
+        where = spots(plane, kind)
+        value = choose(column, rows, sources, [planes[spot] for spot in where] if add else None)
+        for spot, part in zip(where, value):
+            planes[spot] = part
 
     def add_plane(plane, weights, where):
         parts = []
@@ -314,7 +305,7 @@
         for z in (-1, 1):
             plane = 4 + (z > 0)
             sources = [((0, 0, 0), caps[flag(z)]), ((0, 0, z), got[0, 0, z][...])]
-            put(plane, "face", choose(column_of(0, 0, z), edge * edge, sources))
+            put(plane, ("face", 0), column_of(0, 0, z), area, sources)
             add_plane(plane, faces[plane - 2], ("z", last - near(z)))
         arrive([(0, -1, 0), (0, 1, 0)] + [(0, y, z) for y in (-1, 1) for z in (-1, 1)])
         for y in (-1, 1):
@@ -322,7 +313,7 @@
             flat = got[0, y, 0].reshape(edge * edge, slots * c0)
             own = volume[:, line_y(y), :].reshape(edge * edge, slots * c0)
             sources = [((0, 0, 0), own), ((0, y, 0), flat[...])]
-            put(plane, "face", choose(column_of(0, y, 0), edge * edge, sources))
+            put(plane, ("face", 0), column_of(0, y, 0), area, sources)
             for z in (-1, 1):
                 sources = [
                     ((0, 0, 0), lines[flag(z), flag(y)]),
@@ -330,18 +321,18 @@
                     ((0, 0, z), got[0, 0, z][skip(near(y)), :]),
                     ((0, y, z), got[0, y, z][...]),
                 ]
-                put(plane, ("column", beyond(z)), choose(column_of(0, y, z), edge, sources))
+                put(plane, ("column", beyond(z)), column_of(0, y, z), edge, sources)
             add_plane(plane, faces[plane - 2], ("y", (last - near(y)) * edge))
         for x in (-1, 1):
             plane, xe = (x > 0) + 0, near(x)
-            put(plane, "face", choose(column_of(x, 0, 0), edge * edge, [((0, 0, 0), volume[xe])]))
+            put(plane, ("face", 0), column_of(x, 0, 0), area, [((0, 0, 0), volume[xe])])
             for y in (-1, 1):
                 sources = [((0, 0, 0), volume[xe, line_y(y), :]), ((0, y, 0), got[0, y, 0][xe])]
-                put(plane, ("row", beyond(y)), choose(column_of(x, y, 0), edge, sources))
+                put(plane, ("row", beyond(y)), column_of(x, y, 0), edge, sources)
             for z in (-1, 1):
                 span = slice(xe * edge, xe * edge + edge)
                 sources = [((0, 0, 0), caps[flag(z), span, :]), ((0, 0, z), got[0, 0, z][span, :])]
-                put(plane, ("column", beyond(z)), choose(column_of(x, 0, z), edge, sources))
+                put(plane, ("column", beyond(z)), column_of(x, 0, z), edge, sources)
             for y in (-1, 1):
                 for z in (-1, 1):
                     at = xe * edge + near(y)
@@ -351,19 +342,19 @@
                         ((0, 0, z), got[0, 0, z][at : at + 1, :]),
                         ((0, y, z), got[0, y, z][xe : xe + 1, :]),
                     ]
-                    put(plane, ("cell", (beyond(y), beyond(z))), choose(column_of(x, y, z), 1, sources))
-            add_plane(plane, weights[2 * (x > 0)], ("x", (last - xe) * edge * edge))
+                    put(plane, ("cell", (beyond(y), beyond(z))), column_of(x, y, z), 1, sources)
+        add_plane(half, weights[2 * half], ("x", pl.multiple_of(half * last * area, area)))
         arrive([p for p in order_of[::-1] if p[0] == 1])
-        plane = 6
+        plane = 1 - half
         x = 1 - 2 * half
         face = got[1, 0, 0]
-        put(plane, "face", choose(column_of(x, 0, 0), edge * edge, [((1, 0, 0), face[0])]))
+        put(plane, ("face", 0), column_of(x, 0, 0), area, [((1, 0, 0), face[0])], True)
         for y in (-1, 1):
             sources = [((1, 0, 0), face[0, line_y(y), :]), ((1, y, 0), got[1, y, 0][0])]
-            put(plane, ("row", beyond(y)), choose(column_of(x, y, 0), edge, sources))
+            put(plane, ("row", beyond(y)), column_of(x, y, 0), edge, sources, True)
         for z in (-1, 1):
             sources = [((1, 0, 0), face[0, skip(near(z)), :]), ((1, 0, z), got[1, 0, z][...])]
-            put(plane, ("column", beyond(z)), choose(column_of(x, 0, z), edge, sources))
+            put(plane, ("column", beyond(z)), column_of(x, 0, z), edge, sources, True)
         for y in (-1, 1):
             for z in (-1, 1):
                 at = near(y) * edge + near(z)
@@ -373,9 +364,8 @@
                     ((1, 0, z), got[1, 0, z][near(y) : near(y) + 1, :]),
                     ((1, y, z), got[1, y, z][pl.ds(half * last, 1), :]),
                 ]
-                put(plane, ("cell", (beyond(y), beyond(z))), choose(column_of(x, y, z), 1, sources))
-        facing = pl.multiple_of((1 - half) * last * edge * edge, edge * edge)
-        add_plane(plane, weights[2 * (1 - half)], ("x", facing))
+                put(plane, ("cell", (beyond(y), beyond(z))), column_of(x, y, z), 1, sources, True)
+        add_plane(plane, weights[2 * plane], ("x", pl.multiple_of(plane * last * area, area)))
 
     def surface(level):
         volume, caps, lines = level["v"], level["caps"], level["lines"]
@@ -385,7 +375,7 @@
             for j, y in enumerate((0, edge - 1)):
                 line = caps[k, pl.ds(y, edge, stride=edge), :]
                 lines[k, j] = line
-                level["send_l"][k, j] = jnp.concatenate([line, line], axis=0).astype(BF16)
+                level["send_l"][k, j] = line.astype(BF16)
             level["send_z"][k] = caps[k].astype(BF16)
         for j, y in enumerate((0, edge - 1)):
             face = volume[:, y * edge : (y + 1) * edge, :].reshape(area, slots * c0)
@@ -400,41 +390,45 @@
                     at, tap = (3 * i + j) * width, (3 * j + 2 * k) * width
                     target[2 + k, :, at : at + width] = weights[i, :, tap : tap + width]
 
-    taps = wc.shape[1] - 1
+    taps = wc.shape[2] - 1
 
     pairs = n // 2
     pair, core = m // 2, m % 2
     partner = pair * 2 + 1 - core
 
-    def weight_copies(part, role, r):
+    def span(part):
         first, last = (taps + 1) * part // PIECES, (taps + 1) * (part + 1) // PIECES
-        other = (pair + pairs - r) % pairs * 2
-        owner, came = [(m, partner), (m, other + core), (other + core, other + 1 - core)][role]
-        target = (pair + r) % pairs * 2 + core if role == 1 else partner
-        lane = (0, r, pairs - 1 + r)[role]
-
-        def copy(who):
-            spot = wc.at[who, pl.ds(first, last - first)]
-            return pltpu.make_async_remote_copy(
-                src_ref=spot,
-                dst_ref=spot,
-                send_sem=wsend.at[part, lane],
-                recv_sem=wrecv.at[part, lane],
-                device_id=(g, target),
-                device_id_type=MESH,
-            )
-
-        return functools.partial(copy, owner), functools.partial(copy, came)
+        return pl.ds(first, last - first)
+
+    def weight_copy(part, r, owner, target):
+        return pltpu.make_async_remote_copy(
+            src_ref=wc.at[core, owner, span(part)],
+            dst_ref=wc.at[core, owner, span(part)],
+            send_sem=wsend.at[part, r],
+            recv_sem=wrecv.at[part, r],
+            device_id=(g, target * 2 + core),
+            device_id_type=MESH,
+        )
+
+    def share_copy(part, owner_core):
+        return pltpu.make_async_remote_copy(
+            src_ref=wc.at[owner_core, :, span(part)],
+            dst_ref=wc.at[owner_core, :, span(part)],
+            send_sem=wsend.at[part, 0],
+            recv_sem=wrecv.at[part, 0],
+            device_id=(g, partner),
+            device_id_type=MESH,
+        )
 
     def send_weights(part):
         for r in range(1, pairs):
-            weight_copies(part, 1, r)[0]().start()
-        weight_copies(part, 0, 0)[0]().start()
+            weight_copy(part, r, pair, (pair + r) % pairs).start()
 
     def hand_on(part):
         for r in range(1, pairs):
-            weight_copies(part, 1, r)[1]().wait_recv()
-            weight_copies(part, 2, r)[0]().start()
+            other = (pair + pairs - r) % pairs
+            weight_copy(part, r, other, other).wait_recv()
+        share_copy(part, core).start()
 
     def diagonal(matrix):
         empty = jnp.zeros_like(matrix)
@@ -490,7 +484,7 @@
     send(leaf_a)
     loads[4].wait()
     loads[5].wait()
-    wc[m, taps] = jnp.concatenate([wp[...]] * (c1 // c0), axis=1)
+    wc[core, pair, taps] = jnp.concatenate([wp[...]] * (c1 // c0), axis=1)
     send_weights(0)
     loads[0].wait()
     fill_diagonal(w1, b1)
@@ -558,15 +552,23 @@
     send(low)
     loads[3].wait()
     skip_top, skip_bottom = diagonal(wo[:, :c0])
-    lift_top, lift_bottom = diagonal(wo[:, c0:])
     skip_weights = jnp.concatenate([skip_top, skip_bottom], axis=0)
-    lift_weights = jnp.concatenate([lift_top, lift_bottom], axis=0)
     mixed = matmul_nt(skip_weights, second)
     hand_on(2)
     for part in range(PIECES):
-        weight_copies(part, 0, 0)[1]().wait_recv()
-        for r in range(1, pairs):
-            weight_copies(part, 2, r)[1]().wait_recv()
+        share_copy(part, 1 - core).wait_recv()
+    c2 = n * wc.shape[3]
+    rows = slots * cells
+    project = lax.dot_general(
+        wo[:, c0:], wc[:, :, taps].reshape(c2, c1)[:, :c0], (((1,), (1,)), ((), ())), preferred_element_type=F32
+    )
+    high = project.astype(BF16)
+    project = jnp.concatenate([high, (project - high.astype(F32)).astype(BF16)], axis=0)
+    row = lax.broadcasted_iota(jnp.int32, (3 * rows, voxels), 0) % cells
+    column = lax.broadcasted_iota(jnp.int32, (3 * rows, voxels), 1)
+    factor = edge // small
+    x, y, z = column // area, column // edge % edge, column % edge
+    widen = jnp.where(row == (x // factor) * small * small + (y // factor) * small + z // factor, 1.0, 0.0).astype(BF16)
     receive(low)
     sources = [pooled]
     for i, p in enumerate(PARTNERS):
@@ -574,22 +576,19 @@
     spare = gather.shape[1] - len(sources) * slots * cells
     sources.append(jnp.zeros((spare, c1), BF16))
     spread = jnp.dot(gather[...], jnp.concatenate(sources, axis=0), preferred_element_type=F32).astype(BF16)
-    rows = slots * cells
     window = jnp.concatenate([spread[t * rows : (t + 1) * rows] for t in range(taps)], axis=1)
-    c2 = n * wc.shape[2]
-    weights = jnp.concatenate([wc[:, t].reshape(c2, c1) for t in range(taps)], axis=1)
-    total = matmul_nt(window, weights)
-    hidden = rounded_gelu(total)
-    coarse = jnp.dot(hidden, wc[:, taps].reshape(c2, c1)[:, :c0], preferred_element_type=F32)
-    coarse = jnp.concatenate([coarse[b * cells : (b + 1) * cells] for b in range(slots)], axis=1).astype(BF16)
-    row = lax.broadcasted_iota(jnp.int32, (voxels, cells), 0)
-    column = lax.broadcasted_iota(jnp.int32, (voxels, cells), 1)
-    factor = edge // small
-    x, y, z = row // (edge * edge), row // edge % edge, row % edge
-    spread = column == (x // factor) * small * small + (y // factor) * small + z // factor
-    spread = jnp.where(spread, 1.0, 0.0).astype(BF16)
-    widened = jnp.dot(spread, coarse, preferred_element_type=F32).astype(BF16)
-    mixed = mixed + matmul_nt(lift_weights, widened)
+    weights = jnp.concatenate([wc[:, :, t].reshape(c2, c1) for t in range(taps)], axis=1)
+    hidden = rounded_gelu(matmul_nt(weights, jnp.concatenate([window] * 3, axis=0)))
+    lifted = jnp.dot(project, hidden, preferred_element_type=F32)
+    lifted = lifted[:c0] + lifted[c0:]
+    high = lifted.astype(BF16).astype(F32)
+    middle_bits = (lifted - high).astype(BF16).astype(F32)
+    low_bits = lifted - high - middle_bits
+    column = lax.broadcasted_iota(jnp.int32, lifted.shape, 1)
+    terms = jnp.where(column < rows, high, jnp.where(column < 2 * rows, middle_bits, low_bits))
+    owner_of = column % rows // cells
+    terms = jnp.concatenate([jnp.where(owner_of == b, terms, 0.0) for b in range(slots)], axis=0).astype(BF16)
+    mixed = mixed + jnp.dot(terms, widen, preferred_element_type=F32)
     owner = lax.broadcasted_iota(jnp.int32, mixed.shape, 0) // c0
     mixed = jnp.where(owner < live[0], mixed, 0.0).astype(BF16)
     for b in range(slots):
@@ -598,10 +597,9 @@
     sent(mid)
     sent(low)
     for part in range(PIECES):
-        weight_copies(part, 0, 0)[0]().wait_send()
+        share_copy(part, core).wait_send()
         for r in range(1, pairs):
-            weight_copies(part, 1, r)[0]().wait_send()
-            weight_copies(part, 2, r)[0]().wait_send()
+            weight_copy(part, r, pair, (pair + r) % pairs).wait_send()
 
 
 def leaf_scratch(length, lanes):
@@ -618,8 +616,8 @@
         flat=pltpu.VMEM((length**3, lanes), BF16),
         send_y=pltpu.VMEM((2, length**2, lanes), BF16),
         send_z=pltpu.VMEM((2, length**2, lanes), BF16),
-        send_l=pltpu.VMEM((2, 2, 2 * length, lanes), BF16),
-        land=[pltpu.VMEM((length**2 if sum(map(abs, p)) == 1 else 2 * length, lanes), BF16) for p in PARTNERS],
+        send_l=pltpu.VMEM((2, 2, length, lanes), BF16),
+        land=[pltpu.VMEM((length**2 if sum(map(abs, p)) == 1 else length, lanes), BF16) for p in PARTNERS],
         got=[got(p) for p in PARTNERS],
     )
 
@@ -676,7 +674,7 @@
         pltpu.VMEM(w_second.shape, BF16),
         pltpu.VMEM(w_middle.shape, BF16),
         pltpu.VMEM(w_output.shape, BF16),
-        pltpu.VMEM((n, taps + 1) + w_coarse.shape[1:], BF16),
+        pltpu.VMEM((2, n // 2, taps + 1) + w_coarse.shape[1:], BF16),
         pltpu.VMEM(w_project.shape, BF16),
         pltpu.VMEM((3, lanes, 9 * lanes), BF16),
         pltpu.VMEM((3, lanes, 9 * lanes), BF16),
@@ -688,13 +686,13 @@
         pltpu.VMEM(table.shape, BF16),
         pltpu.VMEM((table.shape[0], 3 * 128), BF16),
         pltpu.VMEM((edge + 2,) * 3 + (lanes,), F32),
-        pltpu.VMEM((7, (edge + 2) * 2 * edge, lanes), F32),
+        pltpu.VMEM((6, (edge + 2) * 2 * edge, lanes), F32),
         pltpu.VMEM((edge**3, lanes), F32),
     ]
     sems = [
         pltpu.SemaphoreType.DMA((10,)),
-        pltpu.SemaphoreType.DMA((PIECES, n - 1)),
-        pltpu.SemaphoreType.DMA((PIECES, n - 1)),
+        pltpu.SemaphoreType.DMA((PIECES, n // 2)),
+        pltpu.SemaphoreType.DMA((PIECES, n // 2)),
         pltpu.SemaphoreType.DMA((2, len(PARTNERS))),
         pltpu.SemaphoreType.DMA((2, len(PARTNERS))),
     ]

time: 26.3 us -> 25.6 us (0.973)
  Pallas kernels: 24.8 us -> 24.2 us
    pallas_call x1, Pallas kernels: 24.8 us -> 24.2 us  [shards(): pl.pallas_call(functools.partial(kernel, grps, n), out_shape=pltpu.VMEM(f...]
where the time goes in v3:
time: 25.6 us; the launch traced here: 25.5 us
  Pallas kernels  24.2 us (95%)
  local copies, waits for them, and re-layouts  0.66 us (3%)
  between operations  0.66 us (3%)
    pallas_call x1, Pallas kernels, shards(): pl.pallas_call(functools.partial(kernel, grps, n), out_shape=pltpu.VMEM(f...  24.2 us
    unnamed x1, local copies, waits for them, and re-layouts  0.66 us

profile of v3, /device:TPU:0, one launch (start us, length us, event | category | flops | bytes accessed | tf_op | source)
XLA Modules:
  0.0 25.5 jit_solution(12624201841333431852)
XLA Ops:
  0.7 24.2 %shard_map.100 = bf16[2,64,512]{2,1,0:T(8,128)(2,1)S(1)} custom-call(bf16[2,64,512]{2,1,0:T(8,128)(2,1)} %feat_any.1, s32[1]{0:T(128)S(6)} %copy.13.live_any, s32[2,27]{1,0:T(2,128)} %neigh_any.1, bf16[27,64,64]{2,1,0:T(8,128)(2,1)} %w1_any.1, bf16[27,64,64]{2,1,0:T(8,128)(2,1)} %w2_any.1, bf16[27,64,128]{2,1,0:T(8,128)(2,1)} %bitcast.1, ...), custom_call_target="tpu_custom_call" | custom-call | tf_op jit(solution)/shard_map/pallas_call | solution.py:702
  24.8 0.7 %copy.12 = bf16[2,64,512]{2,1,0:T(8,128)(2,1)} copy(bf16[2,64,512]{2,1,0:T(8,128)(2,1)S(1)} %shard_map.100) | data formatting | bytes 262144

commit v4 on v3

--- a/solution.py
+++ b/solution.py
@@ -22,7 +22,9 @@
 
 
 def rounded_gelu(value):
-    return jax.nn.gelu(value).astype(BF16)
+    scale = (2 / np.pi) ** 0.5
+    half = 0.5 * value
+    return (half + half * jnp.tanh(value * (scale + scale * 0.044715 * (value * value)))).astype(BF16)
 
 
 def kernel(grps, n, feat_any, live_any, neigh_any, w1_any, w2_any, wm_any, wc_any, wp_any, wo_any, table_any, out, levels, mats, live, neigh, sems):
@@ -55,7 +57,7 @@
     (feat, w1, w2, wm, wo, wc, wp, b1, b2, f1, f2, bm, im_leaf, im_mid, table, gather, ext_leaf, planes, acc) = mats
     (local_sem, wsend, wrecv, hsend, hrecv) = sems
     for i, level in enumerate(levels):
-        level.update(send=hsend.at[i % 2], recv=hrecv.at[i % 2])
+        level.update(send=hsend, recv=hrecv.at[i % 2])
     loads = [
         pltpu.make_async_copy(source, target, local_sem.at[i])
         for i, (source, target) in enumerate(
@@ -153,13 +155,14 @@
             def _():
                 copy_to(level, i).wait_recv()
 
-    def extend(level):
+    def extend(level, own):
         volume, ext, caps = level["v"], level["ext"], level["caps"]
         length, lanes = volume.shape[0], volume.shape[3]
         middle = lanes // 2
         lane = lax.broadcasted_iota(jnp.int32, (1, 1, 1, lanes), 3)
         upper = (lane >= middle).astype(jnp.int32)
-        ext[1 : length + 1, 1 : length + 1, 1 : length + 1, :] = volume[...]
+        if own:
+            ext[1 : length + 1, 1 : length + 1, 1 : length + 1, :] = volume[...]
         firsts = {}
         for p in [(0, 0, 0)] + PARTNERS:
             a, b = coords(p)
@@ -178,11 +181,14 @@
             shape = tuple(length if s == 0 else 1 for s in (x, y, z)) + (lanes,)
             wanted = jnp.broadcast_to(wanted, shape)
             upper_full = jnp.broadcast_to(upper, shape)
-            value = jnp.zeros(shape, F32)
+            target = (target_at(x), target_at(y), target_at(z))
+            value = jnp.zeros(shape, F32) if own else ext[target]
             for h in (0, 1) if x else (0,):
                 for cy in (0, y) if y else (0,):
                     for cz in (0, z) if z else (0,):
                         p = (h, cy, cz)
+                        if (p == (0, 0, 0)) != own:
+                            continue
                         at_x = slice(0, 1) if h else source_at(x)
                         at_y = slice(0, 1) if cy else source_at(y)
                         at_z = slice(0, 1) if cz else source_at(z)
@@ -199,7 +205,7 @@
                             found,
                             jnp.where(wanted == firsts[p] + 1 - upper_full, swapped, value),
                         )
-            ext[target_at(x), target_at(y), target_at(z), :] = value
+            ext[target] = value
 
     half_lanes = slots * c0 // 2
     lane = lax.broadcasted_iota(jnp.int32, (edge, slots * c0), 1)
@@ -494,6 +500,7 @@
     loads[7].wait()
     loads[8].wait()
     fill_gather()
+    sent(leaf_a)
     halo(leaf_a, b1, f1)
     first = rounded_gelu(acc[...])
 
@@ -507,7 +514,7 @@
     fill_faces(b2, f2)
     convolve_own(leaf_b, b2)
     hand_on(0)
-    sent(leaf_a)
+    sent(leaf_b)
     halo(leaf_b, b2, f2)
     second = rounded_gelu(acc[...])
 
@@ -530,10 +537,11 @@
     send_weights(2)
     loads[2].wait()
     fill_upright(wm, bm)
+    extend(mid, True)
     hand_on(1)
-    sent(leaf_b)
+    sent(mid)
     receive(mid)
-    extend(mid)
+    extend(mid, False)
     lanes = slots * c0
     for k in range(9):
         ty, tz = k // 3, k % 3
@@ -594,7 +602,6 @@
     for b in range(slots):
         out[b] = mixed[b * c0 : (b + 1) * c0]
 
-    sent(mid)
     sent(low)
     for part in range(PIECES):
         share_copy(part, core).wait_send()
@@ -693,7 +700,7 @@
         pltpu.SemaphoreType.DMA((10,)),
         pltpu.SemaphoreType.DMA((PIECES, n // 2)),
         pltpu.SemaphoreType.DMA((PIECES, n // 2)),
-        pltpu.SemaphoreType.DMA((2, len(PARTNERS))),
+        pltpu.SemaphoreType.DMA((len(PARTNERS),)),
         pltpu.SemaphoreType.DMA((2, len(PARTNERS))),
     ]
     smem = pl.BlockSpec(memory_space=pltpu.SMEM)

time: 25.6 us -> 25.4 us (level)
  Pallas kernels: 24.2 us -> 23.9 us
where the time goes in v4:
time: 25.4 us; the launch traced here: 25.2 us
  Pallas kernels  23.9 us (94%)
  local copies, waits for them, and re-layouts  0.66 us (3%)
  between operations  0.66 us (3%)
    pallas_call x1, Pallas kernels, shards(): pl.pallas_call(functools.partial(kernel, grps, n), out_shape=pltpu.VMEM(f...  23.9 us
    unnamed x1, local copies, waits for them, and re-layouts  0.66 us

profile of v4, /device:TPU:0, one launch (start us, length us, event | category | flops | bytes accessed | tf_op | source)
XLA Modules:
  0.0 25.2 jit_solution(12165972128260977974)
XLA Ops:
  0.7 23.9 %shard_map.100 = bf16[2,64,512]{2,1,0:T(8,128)(2,1)S(1)} custom-call(bf16[2,64,512]{2,1,0:T(8,128)(2,1)} %feat_any.1, s32[1]{0:T(128)S(6)} %copy.13.live_any, s32[2,27]{1,0:T(2,128)} %neigh_any.1, bf16[27,64,64]{2,1,0:T(8,128)(2,1)} %w1_any.1, bf16[27,64,64]{2,1,0:T(8,128)(2,1)} %w2_any.1, bf16[27,64,128]{2,1,0:T(8,128)(2,1)} %bitcast.1, ...), custom_call_target="tpu_custom_call" | custom-call | tf_op jit(solution)/shard_map/pallas_call | solution.py:709
  24.6 0.7 %copy.12 = bf16[2,64,512]{2,1,0:T(8,128)(2,1)} copy(bf16[2,64,512]{2,1,0:T(8,128)(2,1)S(1)} %shard_map.100) | data formatting | bytes 262144

commit v5 on v4

--- a/solution.py
+++ b/solution.py
@@ -89,6 +89,7 @@
         value = level["land"][index][...].astype(F32)
         target = level["got"][index]
         target[...] = value.reshape(target.shape)
+        return value
 
     def piece_of(level, partner):
         if "lines" in level:
@@ -302,15 +303,17 @@
         line_y = lambda y: slice(near(y) * edge, near(y) * edge + edge)
         skip = lambda start: pl.ds(start, edge, stride=edge)
 
+        fresh = {}
+
         def arrive(partners):
             wait_for(level, partners)
             for p in partners:
-                unpack(level, p)
+                fresh[p] = unpack(level, p)
 
         arrive([(0, 0, -1), (0, 0, 1)])
         for z in (-1, 1):
             plane = 4 + (z > 0)
-            sources = [((0, 0, 0), caps[flag(z)]), ((0, 0, z), got[0, 0, z][...])]
+            sources = [((0, 0, 0), caps[flag(z)]), ((0, 0, z), fresh[0, 0, z])]
             put(plane, ("face", 0), column_of(0, 0, z), area, sources)
             add_plane(plane, faces[plane - 2], ("z", last - near(z)))
         arrive([(0, -1, 0), (0, 1, 0)] + [(0, y, z) for y in (-1, 1) for z in (-1, 1)])
@@ -318,14 +321,14 @@
             plane = 2 + (y > 0)
             flat = got[0, y, 0].reshape(edge * edge, slots * c0)
             own = volume[:, line_y(y), :].reshape(edge * edge, slots * c0)
-            sources = [((0, 0, 0), own), ((0, y, 0), flat[...])]
+            sources = [((0, 0, 0), own), ((0, y, 0), fresh[0, y, 0])]
             put(plane, ("face", 0), column_of(0, y, 0), area, sources)
             for z in (-1, 1):
                 sources = [
                     ((0, 0, 0), lines[flag(z), flag(y)]),
                     ((0, y, 0), flat[skip(near(z)), :]),
                     ((0, 0, z), got[0, 0, z][skip(near(y)), :]),
-                    ((0, y, z), got[0, y, z][...]),
+                    ((0, y, z), fresh[0, y, z]),
                 ]
                 put(plane, ("column", beyond(z)), column_of(0, y, z), edge, sources)
             add_plane(plane, faces[plane - 2], ("y", (last - near(y)) * edge))
@@ -354,12 +357,12 @@
         plane = 1 - half
         x = 1 - 2 * half
         face = got[1, 0, 0]
-        put(plane, ("face", 0), column_of(x, 0, 0), area, [((1, 0, 0), face[0])], True)
+        put(plane, ("face", 0), column_of(x, 0, 0), area, [((1, 0, 0), fresh[1, 0, 0])], True)
         for y in (-1, 1):
-            sources = [((1, 0, 0), face[0, line_y(y), :]), ((1, y, 0), got[1, y, 0][0])]
+            sources = [((1, 0, 0), face[0, line_y(y), :]), ((1, y, 0), fresh[1, y, 0])]
             put(plane, ("row", beyond(y)), column_of(x, y, 0), edge, sources, True)
         for z in (-1, 1):
-            sources = [((1, 0, 0), face[0, skip(near(z)), :]), ((1, 0, z), got[1, 0, z][...])]
+            sources = [((1, 0, 0), face[0, skip(near(z)), :]), ((1, 0, z), fresh[1, 0, z])]
             put(plane, ("column", beyond(z)), column_of(x, 0, z), edge, sources, True)
         for y in (-1, 1):
             for z in (-1, 1):

time: 25.4 us -> 25.4 us (level)
  no operation moved by 1% of the time
where the time goes in v5:
time: 25.4 us; the launch traced here: 25.3 us
  Pallas kernels  23.9 us (94%)
  local copies, waits for them, and re-layouts  0.66 us (3%)
  between operations  0.66 us (3%)
    pallas_call x1, Pallas kernels, shards(): pl.pallas_call(functools.partial(kernel, grps, n), out_shape=pltpu.VMEM(f...  23.9 us
    unnamed x1, local copies, waits for them, and re-layouts  0.66 us

profile of v5, /device:TPU:0, one launch (start us, length us, event | category | flops | bytes accessed | tf_op | source)
XLA Modules:
  0.0 25.3 jit_solution(7576440158656161315)
XLA Ops:
  0.7 23.9 %shard_map.100 = bf16[2,64,512]{2,1,0:T(8,128)(2,1)S(1)} custom-call(bf16[2,64,512]{2,1,0:T(8,128)(2,1)} %feat_any.1, s32[1]{0:T(128)S(6)} %copy.13.live_any, s32[2,27]{1,0:T(2,128)} %neigh_any.1, bf16[27,64,64]{2,1,0:T(8,128)(2,1)} %w1_any.1, bf16[27,64,64]{2,1,0:T(8,128)(2,1)} %w2_any.1, bf16[27,64,128]{2,1,0:T(8,128)(2,1)} %bitcast.1, ...), custom_call_target="tpu_custom_call" | custom-call | tf_op jit(solution)/shard_map/pallas_call | solution.py:712
  24.6 0.7 %copy.12 = bf16[2,64,512]{2,1,0:T(8,128)(2,1)} copy(bf16[2,64,512]{2,1,0:T(8,128)(2,1)S(1)} %shard_map.100) | data formatting | bytes 262144
